TPU v7x, 128 devices: a whole 4x4x4 slice. The times are simulated.
128 devices in a mesh: grp: 8 (over z, core), narrow: 16 (over y, x).
Axes of the slice: x: 4, y: 4, z: 4, core: 2. Of those that a mesh axis runs over, the one named last changes fastest.
Arguments:
- panel: bfloat16 [64, 229376], P(None, ('grp', 'narrow')), may hold values from -6 to 6
- tiles: bfloat16 [65536, 128, 128], P(('grp', 'narrow')), may hold values from -0.125 to 0.125
- tile_row: int32 [65536], P(('grp', 'narrow')), may hold values from 0 to 1791, as said below
- tile_col: int32 [65536], P(('grp', 'narrow')), may hold values from 0 to 1791, as said below
- tile_count: int32 [128], P(('grp', 'narrow')), may hold values from 128 to 512, as said below
Outputs:
- filtered: bfloat16 [64, 229376], P(None, ('grp', 'narrow'))
- normal_image: float32 [64, 229376], P(None, ('grp', 'narrow'))
Inputs may be any that keep to these rules, and one draw needn't show every extreme that they name: tile_row of a slot on a device of grp index g lies in g * 224 .. (g + 1) * 224 - 1. tile_col of a slot on a device of grp index g lies in (g - 1) * 224 .. (g + 1) * 224 - 1, and in g * 224 .. for g = 0. `tile_count`: some device holds 512 live slots.
All inputs are finite; a program needn't handle non-finite values.
Results may differ from a plain program's by a relative error of at most 0.009.
Values may be sent and summed in bfloat16 or wider, within the bound.
No kernel may reach another device: no remote copies, remote signals or barrier semaphores. Data moves between devices by JAX's collectives and lax.ppermute only.
A program may use at most 128 MiB of HBM per device.

v0:
```python
import jax
import jax.numpy as jnp
from jax import lax
from jax.sharding import PartitionSpec as P


def shifted(value, axis, steps):
    count = lax.axis_size(axis)
    initial, last = (max(0, -steps), min(count, count - steps))
    return lax.ppermute(value, axis, [(source, source + steps) for source in range(initial, last)])


def body(panel, tiles, tile_row, tile_col, tile_count):
    cols = panel.shape[0]
    tile = tiles.shape[1]
    slots = tiles.shape[0]
    nbd = panel.shape[1] // tile
    nbg = nbd * lax.axis_size("narrow")
    group = lax.axis_index("grp")
    prior_piece = shifted(panel, "grp", 1)
    own_all, prior_all = (
        lax.all_gather(panel, "narrow", axis=1, tiled=True),
        lax.all_gather(prior_piece, "narrow", axis=1, tiled=True),
    )
    both = jnp.concatenate([prior_all, own_all], axis=1).reshape(cols, 2 * nbg, tile)
    local_row = tile_row - group * nbg
    local_col = tile_col - (group - 1) * nbg
    count = tile_count[0]
    block = min(64, slots)
    turns = (count + block - 1) // block

    def pick(start):
        part = lax.dynamic_slice_in_dim(tiles, start, block, 0)
        rowidx = lax.dynamic_slice_in_dim(local_row, start, block, 0)
        colidx = lax.dynamic_slice_in_dim(local_col, start, block, 0)
        live = (start + jnp.arange(block) < count).astype(jnp.float32)
        return (part, rowidx, colidx, live)

    def forward(step, acc):
        part, rowidx, colidx, live = pick(step * block)
        pieces = jnp.take(both, colidx, axis=1)
        prod = jnp.einsum("kti,tji->ktj", pieces, part, preferred_element_type=jnp.float32)
        return acc.at[:, rowidx, :].add(prod * live[None, :, None])

    ystart = jnp.zeros((cols, nbg, tile), jnp.float32)
    row_part = lax.fori_loop(0, turns, forward, ystart).reshape(cols, nbg * tile)
    mine = lax.psum_scatter(row_part, "narrow", scatter_dimension=1, tiled=True)
    filtered = mine.astype(jnp.bfloat16)
    group_rows = lax.all_gather(filtered, "narrow", axis=1, tiled=True)
    group_blocks = group_rows.reshape(cols, nbg, tile)

    def backward(step, acc):
        part, rowidx, colidx, live = pick(step * block)
        pieces = jnp.take(group_blocks, rowidx, axis=1)
        prod = jnp.einsum("ktj,tji->kti", pieces, part, preferred_element_type=jnp.float32)
        return acc.at[:, colidx, :].add(prod * live[None, :, None])

    zstart = jnp.zeros((cols, 2 * nbg, tile), jnp.float32)
    col_part = lax.fori_loop(0, turns, backward, zstart)
    prior_term = col_part[:, :nbg, :].reshape(cols, nbg * tile)
    own_term = col_part[:, nbg:, :].reshape(cols, nbg * tile)
    own_sum, prior_sum = (
        lax.psum_scatter(
            own_term.astype(jnp.bfloat16), "narrow", scatter_dimension=1, tiled=True
        ).astype(jnp.float32),
        lax.psum_scatter(
            prior_term.astype(jnp.bfloat16), "narrow", scatter_dimension=1, tiled=True
        ).astype(jnp.float32),
    )
    from_next = shifted(prior_sum.astype(jnp.bfloat16), "grp", -1).astype(prior_sum.dtype)
    result = own_sum + from_next
    return (filtered, result)


def solution(mesh):
    placed = (
        P(None, ("grp", "narrow")),
        P(("grp", "narrow"), None, None),
        P(("grp", "narrow")),
        P(("grp", "narrow")),
        P(("grp", "narrow")),
    )
    return jax.shard_map(
        body,
        mesh=mesh,
        in_specs=placed,
        out_specs=(P(None, ("grp", "narrow")), P(None, ("grp", "narrow"))),
        check_vma=False,
    )
```

profile of v0, /device:TPU:0, one launch (start us, length us, event | category | flops | bytes accessed | tf_op | source)
XLA Modules:
  0.0 717.0 jit_solution(3994924240693866123)
XLA Ops:
  12.7 49.5 %all-gather.6.cloned.1.call-done = bf16[64,28672]{1,0:T(8,128)(2,1)} async-done(((bf16[64,1792]{1,0:T(8,128)(2,1)}), bf16[64,28672]{1,0:T(8,128)(2,1)}) %all-gather.6.cloned.1.call-update) | async-done | bytes 3670032 | tf_op jit(solution)/shard_map/all_gather | solution.py:22
  62.2 51.4 %all-gather.4.cloned.1.call-done = bf16[64,28672]{1,0:T(8,128)(2,1)} async-done(((bf16[64,1792]{1,0:T(8,128)(2,1)}), bf16[64,28672]{1,0:T(8,128)(2,1)}) %all-gather.4.cloned.1.call-update) | async-done | bytes 3670032 | tf_op jit(solution)/shard_map/all_gather | solution.py:23
  124.5 135.5 %while.20 = (s32[]{:T(128)}, f32[64,224,128]{2,0,1:T(8,128)}, s32[]{:T(128)}, s32[512]{0:T(512)S(1)}, bf16[512,128,128]{2,1,0:T(8,128)(2,1)}, /*index=5*/s32[512...) while((s32[]{:T(128)}, f32[64,224,128]{2,0,1:T(8,128)}, ...), condition=%wide.region_2.3_spmd, body=%wide.region_0.2_spmd.sunk | while | flops 135792384 | bytes 13638199 | solution.py:46
  132.2 9.1 %scatter_fusion = f32[64,224,128]{2,0,1:T(8,128)} fusion(f32[64,224,128]{2,0,1:T(8,128)} %get-tuple-element.281, s32[64]{0:T(128)S(1)} %compare_select_fusion.8, f32[64,64,128]{2,1,0:T(8,128)S(1)} %multiply_bitcast_fusion.4), kind=kCustom, calls=%fused_computation.2.clone.1 | custom fusion | flops 524288 | bytes 6291712 | tf_op jit(solution)/shard_map/while/body/scatter-add | solution.py:43
  149.1 9.2 %scatter_fusion = f32[64,224,128]{2,0,1:T(8,128)} fusion(f32[64,224,128]{2,0,1:T(8,128)} %get-tuple-element.281, s32[64]{0:T(128)S(1)} %compare_select_fusion.8, f32[64,64,128]{2,1,0:T(8,128)S(1)} %multiply_bitcast_fusion.4), kind=kCustom, calls=%fused_computation.2.clone.1 | custom fusion | flops 524288 | bytes 6291712 | tf_op jit(solution)/shard_map/while/body/scatter-add | solution.py:43
  166.1 9.1 %scatter_fusion = f32[64,224,128]{2,0,1:T(8,128)} fusion(f32[64,224,128]{2,0,1:T(8,128)} %get-tuple-element.281, s32[64]{0:T(128)S(1)} %compare_select_fusion.8, f32[64,64,128]{2,1,0:T(8,128)S(1)} %multiply_bitcast_fusion.4), kind=kCustom, calls=%fused_computation.2.clone.1 | custom fusion | flops 524288 | bytes 6291712 | tf_op jit(solution)/shard_map/while/body/scatter-add | solution.py:43
  183.0 9.2 %scatter_fusion = f32[64,224,128]{2,0,1:T(8,128)} fusion(f32[64,224,128]{2,0,1:T(8,128)} %get-tuple-element.281, s32[64]{0:T(128)S(1)} %compare_select_fusion.8, f32[64,64,128]{2,1,0:T(8,128)S(1)} %multiply_bitcast_fusion.4), kind=kCustom, calls=%fused_computation.2.clone.1 | custom fusion | flops 524288 | bytes 6291712 | tf_op jit(solution)/shard_map/while/body/scatter-add | solution.py:43
  199.9 9.2 %scatter_fusion = f32[64,224,128]{2,0,1:T(8,128)} fusion(f32[64,224,128]{2,0,1:T(8,128)} %get-tuple-element.281, s32[64]{0:T(128)S(1)} %compare_select_fusion.8, f32[64,64,128]{2,1,0:T(8,128)S(1)} %multiply_bitcast_fusion.4), kind=kCustom, calls=%fused_computation.2.clone.1 | custom fusion | flops 524288 | bytes 6291712 | tf_op jit(solution)/shard_map/while/body/scatter-add | solution.py:43
  216.9 9.1 %scatter_fusion = f32[64,224,128]{2,0,1:T(8,128)} fusion(f32[64,224,128]{2,0,1:T(8,128)} %get-tuple-element.281, s32[64]{0:T(128)S(1)} %compare_select_fusion.8, f32[64,64,128]{2,1,0:T(8,128)S(1)} %multiply_bitcast_fusion.4), kind=kCustom, calls=%fused_computation.2.clone.1 | custom fusion | flops 524288 | bytes 6291712 | tf_op jit(solution)/shard_map/while/body/scatter-add | solution.py:43
  233.9 9.1 %scatter_fusion = f32[64,224,128]{2,0,1:T(8,128)} fusion(f32[64,224,128]{2,0,1:T(8,128)} %get-tuple-element.281, s32[64]{0:T(128)S(1)} %compare_select_fusion.8, f32[64,64,128]{2,1,0:T(8,128)S(1)} %multiply_bitcast_fusion.4), kind=kCustom, calls=%fused_computation.2.clone.1 | custom fusion | flops 524288 | bytes 6291712 | tf_op jit(solution)/shard_map/while/body/scatter-add | solution.py:43
  250.8 9.2 %scatter_fusion = f32[64,224,128]{2,0,1:T(8,128)} fusion(f32[64,224,128]{2,0,1:T(8,128)} %get-tuple-element.281, s32[64]{0:T(128)S(1)} %compare_select_fusion.8, f32[64,64,128]{2,1,0:T(8,128)S(1)} %multiply_bitcast_fusion.4), kind=kCustom, calls=%fused_computation.2.clone.1 | custom fusion | flops 524288 | bytes 6291712 | tf_op jit(solution)/shard_map/while/body/scatter-add | solution.py:43
  266.5 82.3 %reduce-scatter.4.cloned.1.call-done = f32[64,1792]{1,0:T(8,128)} async-done(((f32[64,28672]{1,0:T(8,128)}), f32[64,1792]{1,0:T(8,128)}) %reduce-scatter.4.cloned.1.call-update) | async-done | bytes 458768 | tf_op jit(solution)/shard_map/reduce_scatter | solution.py:47
  350.6 49.8 %all-gather.8.cloned.1.call-done = bf16[64,28672]{1,0:T(8,128)(2,1)} async-done(((bf16[64,1792]{1,0:T(8,128)(2,1)}), bf16[64,28672]{1,0:T(8,128)(2,1)}) %all-gather.8.cloned.1.call-update) | async-done | bytes 3670032 | tf_op jit(solution)/shard_map/all_gather | solution.py:49
  412.4 120.7 %while.21 = (s32[]{:T(128)}, f32[64,448,128]{2,0,1:T(8,128)}, s32[]{:T(128)}, s32[512]{0:T(512)S(1)}, bf16[512,128,128]{2,1,0:T(8,128)(2,1)}, /*index=5*/s32[512...) while((s32[]{:T(128)}, f32[64,448,128]{2,0,1:T(8,128)}, ...), condition=%wide.region_6.7_spmd, body=%wide.region_4.6_spmd.sunk | while | flops 135792384 | bytes 13638199 | solution.py:59
  418.3 9.1 %scatter_fusion.1 = f32[64,448,128]{2,0,1:T(8,128)} fusion(f32[64,448,128]{2,0,1:T(8,128)} %get-tuple-element.317, s32[64]{0:T(128)S(1)} %compare_select_fusion.9, f32[64,64,128]{2,1,0:T(8,128)S(1)} %multiply_bitcast_fusion.5), kind=kCustom, calls=%fused_computation.3.clone.1 | custom fusion | flops 524288 | bytes 6291712 | tf_op jit(solution)/shard_map/while/body/scatter-add | solution.py:56
  433.4 9.2 %scatter_fusion.1 = f32[64,448,128]{2,0,1:T(8,128)} fusion(f32[64,448,128]{2,0,1:T(8,128)} %get-tuple-element.317, s32[64]{0:T(128)S(1)} %compare_select_fusion.9, f32[64,64,128]{2,1,0:T(8,128)S(1)} %multiply_bitcast_fusion.5), kind=kCustom, calls=%fused_computation.3.clone.1 | custom fusion | flops 524288 | bytes 6291712 | tf_op jit(solution)/shard_map/while/body/scatter-add | solution.py:56
  448.6 9.2 %scatter_fusion.1 = f32[64,448,128]{2,0,1:T(8,128)} fusion(f32[64,448,128]{2,0,1:T(8,128)} %get-tuple-element.317, s32[64]{0:T(128)S(1)} %compare_select_fusion.9, f32[64,64,128]{2,1,0:T(8,128)S(1)} %multiply_bitcast_fusion.5), kind=kCustom, calls=%fused_computation.3.clone.1 | custom fusion | flops 524288 | bytes 6291712 | tf_op jit(solution)/shard_map/while/body/scatter-add | solution.py:56
  463.7 9.2 %scatter_fusion.1 = f32[64,448,128]{2,0,1:T(8,128)} fusion(f32[64,448,128]{2,0,1:T(8,128)} %get-tuple-element.317, s32[64]{0:T(128)S(1)} %compare_select_fusion.9, f32[64,64,128]{2,1,0:T(8,128)S(1)} %multiply_bitcast_fusion.5), kind=kCustom, calls=%fused_computation.3.clone.1 | custom fusion | flops 524288 | bytes 6291712 | tf_op jit(solution)/shard_map/while/body/scatter-add | solution.py:56
  478.8 9.1 %scatter_fusion.1 = f32[64,448,128]{2,0,1:T(8,128)} fusion(f32[64,448,128]{2,0,1:T(8,128)} %get-tuple-element.317, s32[64]{0:T(128)S(1)} %compare_select_fusion.9, f32[64,64,128]{2,1,0:T(8,128)S(1)} %multiply_bitcast_fusion.5), kind=kCustom, calls=%fused_computation.3.clone.1 | custom fusion | flops 524288 | bytes 6291712 | tf_op jit(solution)/shard_map/while/body/scatter-add | solution.py:56
  493.8 9.2 %scatter_fusion.1 = f32[64,448,128]{2,0,1:T(8,128)} fusion(f32[64,448,128]{2,0,1:T(8,128)} %get-tuple-element.317, s32[64]{0:T(128)S(1)} %compare_select_fusion.9, f32[64,64,128]{2,1,0:T(8,128)S(1)} %multiply_bitcast_fusion.5), kind=kCustom, calls=%fused_computation.3.clone.1 | custom fusion | flops 524288 | bytes 6291712 | tf_op jit(solution)/shard_map/while/body/scatter-add | solution.py:56
  509.0 9.1 %scatter_fusion.1 = f32[64,448,128]{2,0,1:T(8,128)} fusion(f32[64,448,128]{2,0,1:T(8,128)} %get-tuple-element.317, s32[64]{0:T(128)S(1)} %compare_select_fusion.9, f32[64,64,128]{2,1,0:T(8,128)S(1)} %multiply_bitcast_fusion.5), kind=kCustom, calls=%fused_computation.3.clone.1 | custom fusion | flops 524288 | bytes 6291712 | tf_op jit(solution)/shard_map/while/body/scatter-add | solution.py:56
  533.1 10.1 %convert.4 = bf16[64,448,128]{2,0,1:T(8,128)(2,1)} convert(f32[64,448,128]{2,0,1:T(8,128)} %get-tuple-element.89) | non-fusion elementwise | flops 3670016 | bytes 22020096 | tf_op jit(solution)/shard_map/convert.1
  557.2 71.5 %reduce-scatter.8.cloned.1.call-done = bf16[64,1792]{1,0:T(8,128)(2,1)} async-done(((bf16[64,28672]{1,0:T(8,128)(2,1)}), bf16[64,1792]{1,0:T(8,128)(2,1)}) %reduce-scatter.8.cloned.1.call-update) | async-done | bytes 229392 | tf_op jit(solution)/shard_map/reduce_scatter | solution.py:66
  629.9 78.5 %reduce-scatter.6.cloned.1.call-done = bf16[64,1792]{1,0:T(8,128)(2,1)} async-done(((bf16[64,28672]{1,0:T(8,128)(2,1)}), bf16[64,1792]{1,0:T(8,128)(2,1)}) %reduce-scatter.6.cloned.1.call-update) | async-done | bytes 229392 | tf_op jit(solution)/shard_map/reduce_scatter | solution.py:63
  (110 shorter events, 171.5 us)
Async XLA Ops:
  7.2 55.1 %all-gather.6.cloned.1.call-start = ((), (), s32[]{:S(2)}) async-start(), calls=%async_computation.4 | async-start | bytes 3899392 | tf_op jit(solution)/shard_map/all_gather | solution.py:22
  7.9 105.7 %all-gather.4.cloned.1.call-start = ((), (), s32[]{:S(2)}) async-start(), calls=%async_computation.3 | async-start | bytes 3899392 | tf_op jit(solution)/shard_map/all_gather | solution.py:23
  7.9 2.6 collective-permute-start
  10.5 0.7 copy-start
  11.3 337.5 %reduce-scatter.4.cloned.1.call-start = ((), (), s32[]{:S(2)}) async-start(), calls=%async_computation.5 | async-start | bytes 7798784 | tf_op jit(solution)/shard_map/reduce_scatter | solution.py:47
  266.5 133.9 %all-gather.8.cloned.1.call-start = ((), (), s32[]{:S(2)}) async-start(), calls=%async_computation.6 | async-start | bytes 3899392 | tf_op jit(solution)/shard_map/all_gather | solution.py:49
  350.6 278.1 %reduce-scatter.8.cloned.1.call-start = ((), (), s32[]{:S(2)}) async-start(), calls=%async_computation.8 | async-start | bytes 3899392 | tf_op jit(solution)/shard_map/reduce_scatter | solution.py:66
  552.5 155.9 %reduce-scatter.6.cloned.1.call-start = ((), (), s32[]{:S(2)}) async-start(), calls=%async_computation.7 | async-start | bytes 3899392 | tf_op jit(solution)/shard_map/reduce_scatter | solution.py:63
  628.6 79.8 %collective-permute-start.1 = (bf16[64,1792]{1,0:T(8,128)(2,1)}, bf16[64,1792]{1,0:T(8,128)(2,1)S(1)}, u32[]{:S(2)}, u32[]{:S(2)}) collective-permute-start(bf16[64,1792]{1,0:T(8,128)(2,1)} %reduce-scatter.8.cloned.1.call-done), channel_id=1, source_target_pairs={{16,0},{32,16},{48,32},{64,48},{80,64},{96,80},{112,96},{17,1},{33... | collective-permute-start | bytes 688136 | tf_op jit(solution)/shard_map/ppermute | solution.py:10
Sparse Core Ops, SparseCore 0:
  10.2 52.0 all-gather.5
  65.0 48.5 all-gather.3
  266.6 82.1 reduce-scatter.3
  351.4 48.9 all-gather.7
  552.6 75.9 reduce-scatter.7
  631.9 76.4 reduce-scatter.5
where the time goes:
time: 724 us; the launch traced here: 717 us
  waiting for transfers between devices  385 us (53%)
  other arithmetic  180 us (25%)
  local copies, waits for them, and re-layouts  89.9 us (12%)
  matrix products  43.7 us (6%)
  between operations  14.8 us (2%)
    reduce_scatter x1, waiting for transfers between devices, body(): mine = lax.psum_scatter(row_part, 'narrow', scatter_dimension=1, tiled=True)  82.3 us
    reduce_scatter x1, waiting for transfers between devices, body(): lax.psum_scatter(own_term.astype(jnp.bfloat16), 'narrow', scatter_dimensi...  78.5 us
    scatter-add x8, other arithmetic, backward(): return acc.at[:, colidx, :].add(prod * live[None, :, None])  73.2 us
    scatter-add x8, other arithmetic, forward(): return acc.at[:, rowidx, :].add(prod * live[None, :, None])  73.2 us
    reduce_scatter x1, waiting for transfers between devices, body(): lax.psum_scatter(prior_term.astype(jnp.bfloat16), 'narrow', scatter_dimen...  71.5 us
    all_gather x1, waiting for transfers between devices, body(): lax.all_gather(prior_piece, 'narrow', axis=1, tiled=True)  51.4 us
    all_gather x1, waiting for transfers between devices, body(): group_rows = lax.all_gather(filtered, 'narrow', axis=1, tiled=True)  49.8 us
    all_gather x1, waiting for transfers between devices, body(): lax.all_gather(panel, 'narrow', axis=1, tiled=True)  49.5 us
  transfers between devices with their start and end apart: 8, of which 7 were waited for; matrix products, arithmetic and copies ran while one was open for 1% of the time, Pallas kernels for 0%

commit v1 on v0

--- a/solution.py
+++ b/solution.py
@@ -46,7 +46,9 @@
     row_part = lax.fori_loop(0, turns, forward, ystart).reshape(cols, nbg * tile)
     mine = lax.psum_scatter(row_part, "narrow", scatter_dimension=1, tiled=True)
     filtered = mine.astype(jnp.bfloat16)
-    group_rows = lax.all_gather(filtered, "narrow", axis=1, tiled=True)
+    group_rows = jnp.concatenate(
+        lax.all_to_all(jnp.stack([filtered] * lax.axis_size("narrow")), "narrow", 0, 0), axis=1
+    )
     group_blocks = group_rows.reshape(cols, nbg, tile)
 
     def backward(step, acc):

time: 724 us -> 747 us (1.032)
  local copies, waits for them, and re-layouts: 89.9 us -> 106 us
    all_to_all x0 -> x1, waiting for transfers between devices: none -> 52.1 us  [body(): lax.all_to_all(jnp.stack([filtered] * lax.axis_size('narrow')), 'narrow',...]
    all_gather x1 -> x0, waiting for transfers between devices: 49.8 us -> none  [body(): group_rows = lax.all_gather(filtered, 'narrow', axis=1, tiled=True)]
    another operation x0 -> x2, local copies, waits for them, and re-layouts: none -> 10.2 us  [the longest x1 8.03 us: body(): group_blocks = group_rows.reshape(cols, nbg, tile)]
where the time goes in v1:
time: 747 us; the launch traced here: 739 us
  waiting for transfers between devices  387 us (52%)
  other arithmetic  180 us (24%)
  local copies, waits for them, and re-layouts  106 us (14%)
  matrix products  43.7 us (6%)
  between operations  14.5 us (2%)
  starting transfers between devices  7.77 us (1%)
    reduce_scatter x1, waiting for transfers between devices, body(): mine = lax.psum_scatter(row_part, 'narrow', scatter_dimension=1, tiled=True)  82.4 us
    reduce_scatter x1, waiting for transfers between devices, body(): lax.psum_scatter(own_term.astype(jnp.bfloat16), 'narrow', scatter_dimensi...  78.5 us
    scatter-add x8, other arithmetic, backward(): return acc.at[:, colidx, :].add(prod * live[None, :, None])  73.2 us
    scatter-add x8, other arithmetic, forward(): return acc.at[:, rowidx, :].add(prod * live[None, :, None])  73.2 us
    reduce_scatter x1, waiting for transfers between devices, body(): lax.psum_scatter(prior_term.astype(jnp.bfloat16), 'narrow', scatter_dimen...  70.6 us
    all_to_all x1, waiting for transfers between devices, body(): lax.all_to_all(jnp.stack([filtered] * lax.axis_size('narrow')), 'narrow',...  52.1 us
    all_gather x1, waiting for transfers between devices, body(): lax.all_gather(prior_piece, 'narrow', axis=1, tiled=True)  51.4 us
    all_gather x1, waiting for transfers between devices, body(): lax.all_gather(panel, 'narrow', axis=1, tiled=True)  49.5 us
  transfers between devices with their start and end apart: 8, of which 7 were waited for; matrix products, arithmetic and copies ran while one was open for 1% of the time, Pallas kernels for 0%

profile of v1, /device:TPU:0, one launch (start us, length us, event | category | flops | bytes accessed | tf_op | source)
XLA Modules:
  0.0 739.0 jit_solution(8874654010258004688)
XLA Ops:
  12.7 49.5 %all-gather.5.cloned.1.call-done = bf16[64,28672]{1,0:T(8,128)(2,1)} async-done(((bf16[64,1792]{1,0:T(8,128)(2,1)}), bf16[64,28672]{1,0:T(8,128)(2,1)}) %all-gather.5.cloned.1.call-update) | async-done | bytes 3670032 | tf_op jit(solution)/shard_map/all_gather | solution.py:22
  62.2 51.4 %all-gather.3.cloned.1.call-done = bf16[64,28672]{1,0:T(8,128)(2,1)} async-done(((bf16[64,1792]{1,0:T(8,128)(2,1)}), bf16[64,28672]{1,0:T(8,128)(2,1)}) %all-gather.3.cloned.1.call-update) | async-done | bytes 3670032 | tf_op jit(solution)/shard_map/all_gather | solution.py:23
  124.5 135.5 %while.20 = (s32[]{:T(128)}, f32[64,224,128]{2,0,1:T(8,128)}, s32[]{:T(128)}, s32[512]{0:T(512)S(1)}, bf16[512,128,128]{2,1,0:T(8,128)(2,1)}, /*index=5*/s32[512...) while((s32[]{:T(128)}, f32[64,224,128]{2,0,1:T(8,128)}, ...), condition=%wide.region_2.3_spmd, body=%wide.region_0.2_spmd.sunk | while | flops 135792384 | bytes 13638199 | solution.py:46
  132.2 9.1 %scatter_fusion = f32[64,224,128]{2,0,1:T(8,128)} fusion(f32[64,224,128]{2,0,1:T(8,128)} %get-tuple-element.289, s32[64]{0:T(128)S(1)} %compare_select_fusion.8, f32[64,64,128]{2,1,0:T(8,128)S(1)} %multiply_bitcast_fusion.4), kind=kCustom, calls=%fused_computation.2.clone.1 | custom fusion | flops 524288 | bytes 6291712 | tf_op jit(solution)/shard_map/while/body/scatter-add | solution.py:43
  149.1 9.2 %scatter_fusion = f32[64,224,128]{2,0,1:T(8,128)} fusion(f32[64,224,128]{2,0,1:T(8,128)} %get-tuple-element.289, s32[64]{0:T(128)S(1)} %compare_select_fusion.8, f32[64,64,128]{2,1,0:T(8,128)S(1)} %multiply_bitcast_fusion.4), kind=kCustom, calls=%fused_computation.2.clone.1 | custom fusion | flops 524288 | bytes 6291712 | tf_op jit(solution)/shard_map/while/body/scatter-add | solution.py:43
  166.1 9.1 %scatter_fusion = f32[64,224,128]{2,0,1:T(8,128)} fusion(f32[64,224,128]{2,0,1:T(8,128)} %get-tuple-element.289, s32[64]{0:T(128)S(1)} %compare_select_fusion.8, f32[64,64,128]{2,1,0:T(8,128)S(1)} %multiply_bitcast_fusion.4), kind=kCustom, calls=%fused_computation.2.clone.1 | custom fusion | flops 524288 | bytes 6291712 | tf_op jit(solution)/shard_map/while/body/scatter-add | solution.py:43
  183.0 9.2 %scatter_fusion = f32[64,224,128]{2,0,1:T(8,128)} fusion(f32[64,224,128]{2,0,1:T(8,128)} %get-tuple-element.289, s32[64]{0:T(128)S(1)} %compare_select_fusion.8, f32[64,64,128]{2,1,0:T(8,128)S(1)} %multiply_bitcast_fusion.4), kind=kCustom, calls=%fused_computation.2.clone.1 | custom fusion | flops 524288 | bytes 6291712 | tf_op jit(solution)/shard_map/while/body/scatter-add | solution.py:43
  199.9 9.2 %scatter_fusion = f32[64,224,128]{2,0,1:T(8,128)} fusion(f32[64,224,128]{2,0,1:T(8,128)} %get-tuple-element.289, s32[64]{0:T(128)S(1)} %compare_select_fusion.8, f32[64,64,128]{2,1,0:T(8,128)S(1)} %multiply_bitcast_fusion.4), kind=kCustom, calls=%fused_computation.2.clone.1 | custom fusion | flops 524288 | bytes 6291712 | tf_op jit(solution)/shard_map/while/body/scatter-add | solution.py:43
  216.9 9.1 %scatter_fusion = f32[64,224,128]{2,0,1:T(8,128)} fusion(f32[64,224,128]{2,0,1:T(8,128)} %get-tuple-element.289, s32[64]{0:T(128)S(1)} %compare_select_fusion.8, f32[64,64,128]{2,1,0:T(8,128)S(1)} %multiply_bitcast_fusion.4), kind=kCustom, calls=%fused_computation.2.clone.1 | custom fusion | flops 524288 | bytes 6291712 | tf_op jit(solution)/shard_map/while/body/scatter-add | solution.py:43
  233.8 9.1 %scatter_fusion = f32[64,224,128]{2,0,1:T(8,128)} fusion(f32[64,224,128]{2,0,1:T(8,128)} %get-tuple-element.289, s32[64]{0:T(128)S(1)} %compare_select_fusion.8, f32[64,64,128]{2,1,0:T(8,128)S(1)} %multiply_bitcast_fusion.4), kind=kCustom, calls=%fused_computation.2.clone.1 | custom fusion | flops 524288 | bytes 6291712 | tf_op jit(solution)/shard_map/while/body/scatter-add | solution.py:43
  250.8 9.2 %scatter_fusion = f32[64,224,128]{2,0,1:T(8,128)} fusion(f32[64,224,128]{2,0,1:T(8,128)} %get-tuple-element.289, s32[64]{0:T(128)S(1)} %compare_select_fusion.8, f32[64,64,128]{2,1,0:T(8,128)S(1)} %multiply_bitcast_fusion.4), kind=kCustom, calls=%fused_computation.2.clone.1 | custom fusion | flops 524288 | bytes 6291712 | tf_op jit(solution)/shard_map/while/body/scatter-add | solution.py:43
  266.5 82.4 %reduce-scatter.4.cloned.1.call-done = f32[64,1792]{1,0:T(8,128)} async-done(((f32[64,28672]{1,0:T(8,128)}), f32[64,1792]{1,0:T(8,128)}) %reduce-scatter.4.cloned.1.call-update) | async-done | bytes 458768 | tf_op jit(solution)/shard_map/reduce_scatter | solution.py:47
  357.2 52.1 %all-to-all-done = bf16[16,64,1792]{2,1,0:T(8,128)(2,1)} async-done(((bf16[16,64,1792]{2,1,0:T(8,128)(2,1)}), bf16[16,64,1792]{2,1,0:T(8,128)(2,1)}, u32[]{:S(2)}, u32[]{:S(2)}) %all-to-all-start) | async-done | bytes 3670048 | tf_op jit(solution)/shard_map/all_to_all | solution.py:50
  435.6 120.7 %while.21 = (s32[]{:T(128)}, f32[64,448,128]{2,0,1:T(8,128)}, s32[]{:T(128)}, s32[512]{0:T(512)S(1)}, bf16[512,128,128]{2,1,0:T(8,128)(2,1)}, /*index=5*/s32[512...) while((s32[]{:T(128)}, f32[64,448,128]{2,0,1:T(8,128)}, ...), condition=%wide.region_6.7_spmd, body=%wide.region_4.6_spmd.sunk | while | flops 135792384 | bytes 13638199 | solution.py:61
  441.5 9.1 %scatter_fusion.1 = f32[64,448,128]{2,0,1:T(8,128)} fusion(f32[64,448,128]{2,0,1:T(8,128)} %get-tuple-element.325, s32[64]{0:T(128)S(1)} %compare_select_fusion.9, f32[64,64,128]{2,1,0:T(8,128)S(1)} %multiply_bitcast_fusion.5), kind=kCustom, calls=%fused_computation.3.clone.1 | custom fusion | flops 524288 | bytes 6291712 | tf_op jit(solution)/shard_map/while/body/scatter-add | solution.py:58
  456.6 9.2 %scatter_fusion.1 = f32[64,448,128]{2,0,1:T(8,128)} fusion(f32[64,448,128]{2,0,1:T(8,128)} %get-tuple-element.325, s32[64]{0:T(128)S(1)} %compare_select_fusion.9, f32[64,64,128]{2,1,0:T(8,128)S(1)} %multiply_bitcast_fusion.5), kind=kCustom, calls=%fused_computation.3.clone.1 | custom fusion | flops 524288 | bytes 6291712 | tf_op jit(solution)/shard_map/while/body/scatter-add | solution.py:58
  471.7 9.2 %scatter_fusion.1 = f32[64,448,128]{2,0,1:T(8,128)} fusion(f32[64,448,128]{2,0,1:T(8,128)} %get-tuple-element.325, s32[64]{0:T(128)S(1)} %compare_select_fusion.9, f32[64,64,128]{2,1,0:T(8,128)S(1)} %multiply_bitcast_fusion.5), kind=kCustom, calls=%fused_computation.3.clone.1 | custom fusion | flops 524288 | bytes 6291712 | tf_op jit(solution)/shard_map/while/body/scatter-add | solution.py:58
  486.8 9.2 %scatter_fusion.1 = f32[64,448,128]{2,0,1:T(8,128)} fusion(f32[64,448,128]{2,0,1:T(8,128)} %get-tuple-element.325, s32[64]{0:T(128)S(1)} %compare_select_fusion.9, f32[64,64,128]{2,1,0:T(8,128)S(1)} %multiply_bitcast_fusion.5), kind=kCustom, calls=%fused_computation.3.clone.1 | custom fusion | flops 524288 | bytes 6291712 | tf_op jit(solution)/shard_map/while/body/scatter-add | solution.py:58
  501.9 9.1 %scatter_fusion.1 = f32[64,448,128]{2,0,1:T(8,128)} fusion(f32[64,448,128]{2,0,1:T(8,128)} %get-tuple-element.325, s32[64]{0:T(128)S(1)} %compare_select_fusion.9, f32[64,64,128]{2,1,0:T(8,128)S(1)} %multiply_bitcast_fusion.5), kind=kCustom, calls=%fused_computation.3.clone.1 | custom fusion | flops 524288 | bytes 6291712 | tf_op jit(solution)/shard_map/while/body/scatter-add | solution.py:58
  517.0 9.2 %scatter_fusion.1 = f32[64,448,128]{2,0,1:T(8,128)} fusion(f32[64,448,128]{2,0,1:T(8,128)} %get-tuple-element.325, s32[64]{0:T(128)S(1)} %compare_select_fusion.9, f32[64,64,128]{2,1,0:T(8,128)S(1)} %multiply_bitcast_fusion.5), kind=kCustom, calls=%fused_computation.3.clone.1 | custom fusion | flops 524288 | bytes 6291712 | tf_op jit(solution)/shard_map/while/body/scatter-add | solution.py:58
  532.2 9.1 %scatter_fusion.1 = f32[64,448,128]{2,0,1:T(8,128)} fusion(f32[64,448,128]{2,0,1:T(8,128)} %get-tuple-element.325, s32[64]{0:T(128)S(1)} %compare_select_fusion.9, f32[64,64,128]{2,1,0:T(8,128)S(1)} %multiply_bitcast_fusion.5), kind=kCustom, calls=%fused_computation.3.clone.1 | custom fusion | flops 524288 | bytes 6291712 | tf_op jit(solution)/shard_map/while/body/scatter-add | solution.py:58
  556.3 10.1 %convert.4 = bf16[64,448,128]{2,0,1:T(8,128)(2,1)} convert(f32[64,448,128]{2,0,1:T(8,128)} %get-tuple-element.89) | non-fusion elementwise | flops 3670016 | bytes 22020096 | tf_op jit(solution)/shard_map/convert.1
  580.4 70.6 %reduce-scatter.8.cloned.1.call-done = bf16[64,1792]{1,0:T(8,128)(2,1)} async-done(((bf16[64,28672]{1,0:T(8,128)(2,1)}), bf16[64,1792]{1,0:T(8,128)(2,1)}) %reduce-scatter.8.cloned.1.call-update) | async-done | bytes 229392 | tf_op jit(solution)/shard_map/reduce_scatter | solution.py:68
  652.2 78.5 %reduce-scatter.6.cloned.1.call-done = bf16[64,1792]{1,0:T(8,128)(2,1)} async-done(((bf16[64,28672]{1,0:T(8,128)(2,1)}), bf16[64,1792]{1,0:T(8,128)(2,1)}) %reduce-scatter.6.cloned.1.call-update) | async-done | bytes 229392 | tf_op jit(solution)/shard_map/reduce_scatter | solution.py:65
  (114 shorter events, 192.3 us)
Async XLA Ops:
  7.2 55.1 %all-gather.5.cloned.1.call-start = ((), (), s32[]{:S(2)}) async-start(), calls=%async_computation.5 | async-start | bytes 3899392 | tf_op jit(solution)/shard_map/all_gather | solution.py:22
  7.9 105.7 %all-gather.3.cloned.1.call-start = ((), (), s32[]{:S(2)}) async-start(), calls=%async_computation.4 | async-start | bytes 3899392 | tf_op jit(solution)/shard_map/all_gather | solution.py:23
  7.9 2.6 collective-permute-start
  10.5 0.7 copy-start.1
  11.3 337.6 %reduce-scatter.4.cloned.1.call-start = ((), (), s32[]{:S(2)}) async-start(), calls=%async_computation.6 | async-start | bytes 7798784 | tf_op jit(solution)/shard_map/reduce_scatter | solution.py:47
  349.9 65.3 %copy-start = (bf16[64,1792]{1,0:T(8,128)(2,1)}, bf16[64,1792]{1,0:T(8,128)(2,1)S(1)}, u32[]{:S(2)}) copy-start(bf16[64,1792]{1,0:T(8,128)(2,1)S(1)} %convert_element_type.33) | copy-start | bytes 688132
  352.1 57.2 %all-to-all-start = ((bf16[16,64,1792]{2,1,0:T(8,128)(2,1)}), bf16[16,64,1792]{2,1,0:T(8,128)(2,1)}, u32[]{:S(2)}, u32[]{:S(2)}) async-start(bf16[16,64,1792]{2,1,0:T(8,128)(2,1)} %stack.2), calls=%async_computation.1 | async-start | bytes 7340032 | tf_op jit(solution)/shard_map/all_to_all | solution.py:50
  357.1 293.8 %reduce-scatter.8.cloned.1.call-start = ((), (), s32[]{:S(2)}) async-start(), calls=%async_computation.8 | async-start | bytes 3899392 | tf_op jit(solution)/shard_map/reduce_scatter | solution.py:68
  575.7 155.1 %reduce-scatter.6.cloned.1.call-start = ((), (), s32[]{:S(2)}) async-start(), calls=%async_computation.7 | async-start | bytes 3899392 | tf_op jit(solution)/shard_map/reduce_scatter | solution.py:65
  650.9 79.8 %collective-permute-start.1 = (bf16[64,1792]{1,0:T(8,128)(2,1)}, bf16[64,1792]{1,0:T(8,128)(2,1)S(1)}, u32[]{:S(2)}, u32[]{:S(2)}) collective-permute-start(bf16[64,1792]{1,0:T(8,128)(2,1)} %reduce-scatter.8.cloned.1.call-done), channel_id=1, source_target_pairs={{16,0},{32,16},{48,32},{64,48},{80,64},{96,80},{112,96},{17,1},{33... | collective-permute-start | bytes 688136 | tf_op jit(solution)/shard_map/ppermute | solution.py:10
Sparse Core Ops, SparseCore 0:
  10.2 52.0 all-gather.4
  65.0 48.5 all-gather.2
  266.6 82.2 reduce-scatter.3
  575.8 75.0 reduce-scatter.7
  654.1 76.5 reduce-scatter.5
